TPU v7x, 32 devices: a whole 2x2x4 slice. The times are simulated.
32 devices in a mesh: seq: 8 (over z, x), head: 4 (over y, core).
Axes of the slice: x: 2, y: 2, z: 4, core: 2. Of those that a mesh axis runs over, the one named last changes fastest.
Arguments:
- queries: bfloat16 [2048, 2048], P('seq', 'head'), may hold values from -1.75 to 1.75
- keys: bfloat16 [2048, 2048], P('seq', 'head'), may hold values from -1.75 to 1.75
- values: bfloat16 [2048, 2048], P('seq', 'head'), may hold values from -6 to 6
- level_table: float32 [16, 16], P(None, 'head'), may hold values from 0.05 to 1
- level_code: int32 [2048, 6], P('seq'), may hold values from 0 to 15
- out_weight: bfloat16 [2048, 2048], P('head'), may hold values from -0.125 to 0.125
- cotangent: bfloat16 [2048, 2048], P('seq', 'head'), may hold values from -8 to 8
Outputs:
- mixed: bfloat16 [2048, 2048], P('seq', 'head')
- out_weight_grad: float32 [2048, 2048], P('seq', 'head')
- query_grad: bfloat16 [2048, 2048], P('seq', 'head')
- key_grad: bfloat16 [2048, 2048], P('seq', 'head')
- value_grad: bfloat16 [2048, 2048], P('seq', 'head')
- table_grad: float32 [16, 16], P(None, 'head')
All inputs are finite; a program needn't handle non-finite values.
Results may differ from a plain program's by a relative error of at most 0.015.
Values may be sent and summed in bfloat16 or wider, within the bound.
No kernel may reach another device: no remote copies, remote signals or barrier semaphores. Data moves between devices by JAX's collectives and lax.ppermute only.
A program may use at most 128 MiB of HBM per device.

v0:
```python
import math
import jax
import jax.numpy as jnp
from jax import lax
from jax.sharding import PartitionSpec as P

SPAN = 64
HIGHEST_PRECISION = lax.Precision.HIGHEST


def partner_2(value, axis, apart):
    mask = 2**apart
    pairs = [(source, source ^ mask) for source in range(lax.axis_size(axis))]
    return lax.ppermute(value, axis, pairs)


def split_einsum(form, left, right):
    if left.dtype == jnp.float32:
        high = left.astype(jnp.bfloat16)
        rest = (left - high.astype(jnp.float32)).astype(jnp.bfloat16)
        return jnp.einsum(form, high, right, preferred_element_type=jnp.float32) + jnp.einsum(
            form, rest, right, preferred_element_type=jnp.float32
        )
    high = right.astype(jnp.bfloat16)
    rest = (right - high.astype(jnp.float32)).astype(jnp.bfloat16)
    return jnp.einsum(form, left, high, preferred_element_type=jnp.float32) + jnp.einsum(
        form, left, rest, preferred_element_type=jnp.float32
    )


def upper_half(array, bit_index):
    group_size = 2 ** (bit_index + 1)
    grouped = array.reshape((array.shape[0] // group_size, group_size) + array.shape[1:])
    return grouped[:, group_size // 2 :]


def lower_sum(array, bit_index):
    group_size = 2 ** (bit_index + 1)
    grouped = array.reshape((array.shape[0] // group_size, group_size) + array.shape[1:])
    return jnp.sum(grouped[:, : group_size // 2], axis=1)


def place_upper(piece_array, bit_index):
    group_size = 2 ** (bit_index + 1)
    joined = jnp.concatenate([jnp.zeros_like(piece_array), piece_array], axis=1)
    return joined.reshape((piece_array.shape[0] * group_size,) + piece_array.shape[2:])


def spread_lower(piece_array, bit_index):
    group_size = 2 ** (bit_index + 1)
    filled = jnp.broadcast_to(
        piece_array[:, None], (piece_array.shape[0], group_size // 2) + piece_array.shape[1:]
    )
    joined = jnp.concatenate([filled, jnp.zeros_like(filled)], axis=1)
    return joined.reshape((piece_array.shape[0] * group_size,) + piece_array.shape[1:])


def lower_blocks(device_state, position, seq_bits):
    block_state = device_state
    found_states = []
    for bit_index in range(seq_bits):
        partner = partner_2(block_state.astype(jnp.bfloat16), "seq", bit_index).astype(
            block_state.dtype
        )
        bit_owned = (position >> bit_index & 1).astype(jnp.float32)
        found_states.append(partner * bit_owned)
        block_state = block_state + partner
    return found_states


def upper_blocks(device_terms, position, seq_bits):
    stacked_terms = device_terms
    gathered = jnp.zeros_like(device_terms[0])
    for bit_index in range(seq_bits):
        partner = partner_2(stacked_terms.astype(jnp.bfloat16), "seq", bit_index).astype(
            stacked_terms.dtype
        )
        bit_owned = (position >> bit_index & 1).astype(jnp.float32)
        gathered = gathered + (1.0 - bit_owned) * partner[0]
        stacked_terms = stacked_terms[1:] + partner[1:]
    return gathered


def per_device(queries, keys, values, level_table, level_code, out_weight, cotangent):
    tok_rows = queries.shape[0]
    heads_here = level_table.shape[1]
    head_size = queries.shape[1] // heads_here
    span_len = SPAN
    spans_here = tok_rows // span_len
    local_bits = spans_here.bit_length() - 1
    seq_count = lax.axis_size("seq")
    seq_bits = seq_count.bit_length() - 1
    level_count = 1 + local_bits + seq_bits
    position = lax.axis_index("seq")
    four_shape = (spans_here, span_len, heads_here, head_size)
    scales = [
        1.0 / math.sqrt(span_len * 2 ** max(level_index - 1, 0))
        for level_index in range(level_count)
    ]
    code_count = level_table.shape[0]
    one_hot = (
        level_code[:, :, None] == jnp.arange(code_count, dtype=jnp.int32)[None, None, :]
    ).astype(jnp.float32)
    lookup = jnp.einsum("tlc,ch->tlh", one_hot, level_table, precision=HIGHEST_PRECISION)
    lookup = lookup.reshape(spans_here, span_len, level_count, heads_here)
    level_coef = lookup * jnp.asarray(scales, jnp.float32)[None, None, :, None]
    full_rows = lax.all_gather(cotangent, "head", axis=1, tiled=True)
    grad_attn = jnp.einsum(
        "tj,ij->ti", full_rows, out_weight, preferred_element_type=jnp.float32
    ).astype(jnp.bfloat16)
    q_half = queries.reshape(four_shape)
    k_half = keys.reshape(four_shape)
    v_half = values.reshape(four_shape)
    g_half = grad_attn.reshape(four_shape)
    causal = (jnp.arange(span_len)[:, None] >= jnp.arange(span_len)[None, :]).astype(jnp.float32)
    scores = (
        jnp.einsum("jchd,jshd->jhcs", q_half, k_half, preferred_element_type=jnp.float32) * causal
    )
    level_reads = [split_einsum("jhcs,jshe->jche", scores, v_half) * scales[0]]
    span_states = jnp.einsum("jchd,jche->jhde", k_half, v_half, preferred_element_type=jnp.float32)
    local_lower = []
    for bit_index in range(local_bits):
        lower_state = lower_sum(span_states, bit_index)
        local_lower.append(lower_state)
        upper_reads = split_einsum("gjchd,ghde->gjche", upper_half(q_half, bit_index), lower_state)
        level_reads.append(place_upper(upper_reads, bit_index) * scales[1 + bit_index])
    device_state = jnp.sum(span_states, axis=0)
    scaled_seq = g_half[:, :, None] * level_coef[:, :, 1 + local_bits :, :, None]
    device_terms = split_einsum("jchd,jclhe->lhde", q_half, scaled_seq)
    found_states = lower_blocks(device_state, position, seq_bits)
    gathered = upper_blocks(device_terms, position, seq_bits)
    for bit_index in range(seq_bits):
        level_reads.append(
            split_einsum("jchd,hde->jche", q_half, found_states[bit_index])
            * scales[1 + local_bits + bit_index]
        )
    attention = jnp.zeros(four_shape, jnp.float32)
    for level_index in range(level_count):
        attention = attention + lookup[:, :, level_index, :, None] * level_reads[level_index]
    attn_rows = attention.reshape(tok_rows, heads_here * head_size).astype(jnp.bfloat16)
    partial_value = jnp.dot(attn_rows, out_weight, preferred_element_type=jnp.float32)
    mixed = lax.psum_scatter(
        partial_value.astype(jnp.bfloat16), "head", scatter_dimension=1, tiled=True
    )
    weight_norm = 1.0 / math.sqrt(tok_rows * seq_count)
    out_weight_grad = lax.psum_scatter(
        jnp.einsum("tj,ti->ji", full_rows, attn_rows, preferred_element_type=jnp.float32)
        * weight_norm,
        "seq",
        scatter_dimension=0,
        tiled=True,
    )
    level_grads = jnp.stack(
        [jnp.sum(g_half * level_reads[level_index], axis=3) for level_index in range(level_count)],
        axis=2,
    )
    table_norm = 1.0 / math.sqrt(tok_rows * seq_count * level_count)
    table_part = (
        jnp.einsum(
            "tlc,tlh->ch",
            one_hot,
            level_grads.reshape(tok_rows, level_count, heads_here),
            precision=HIGHEST_PRECISION,
        )
        * table_norm
    )
    table_grad = lax.psum(table_part, "seq")
    within_coef = jnp.transpose(level_coef[:, :, 0, :], (0, 2, 1))[:, :, :, None]
    score_grads = (
        jnp.einsum("jche,jshe->jhcs", g_half, v_half, preferred_element_type=jnp.float32)
        * causal
        * within_coef
    )
    query_grad = split_einsum("jhcs,jshd->jchd", score_grads, k_half)
    key_grad = split_einsum("jhcs,jchd->jshd", score_grads, q_half)
    value_grad = split_einsum("jhcs,jche->jshe", scores * within_coef, g_half)
    upper_terms = jnp.zeros_like(span_states)
    for bit_index in range(local_bits):
        coef_here = level_coef[:, :, 1 + bit_index, :, None]
        query_part = upper_half(coef_here, bit_index) * split_einsum(
            "gjche,ghde->gjchd", upper_half(g_half, bit_index), local_lower[bit_index]
        )
        query_grad = query_grad + place_upper(query_part, bit_index)
        scaled_grads = upper_half(g_half * coef_here, bit_index)
        block_terms = split_einsum("gjchd,gjche->ghde", upper_half(q_half, bit_index), scaled_grads)
        upper_terms = upper_terms + spread_lower(block_terms, bit_index)
    for bit_index in range(seq_bits):
        coef_here = level_coef[:, :, 1 + local_bits + bit_index, :, None]
        query_grad = query_grad + coef_here * split_einsum(
            "jche,hde->jchd", g_half, found_states[bit_index]
        )
    states_back = upper_terms + gathered[None]
    key_grad = key_grad + split_einsum("jhde,jche->jchd", states_back, v_half)
    value_grad = value_grad + split_einsum("jhde,jchd->jche", states_back, k_half)
    flat_shape = (tok_rows, heads_here * head_size)
    return (
        mixed,
        out_weight_grad,
        query_grad.reshape(flat_shape).astype(jnp.bfloat16),
        key_grad.reshape(flat_shape).astype(jnp.bfloat16),
        value_grad.reshape(flat_shape).astype(jnp.bfloat16),
        table_grad,
    )


def solution(mesh):
    placed = (
        P("seq", "head"),
        P("seq", "head"),
        P("seq", "head"),
        P(None, "head"),
        P("seq", None),
        P("head", None),
        P("seq", "head"),
    )
    return jax.shard_map(
        per_device,
        mesh=mesh,
        in_specs=placed,
        out_specs=(
            P("seq", "head"),
            P("seq", "head"),
            P("seq", "head"),
            P("seq", "head"),
            P("seq", "head"),
            P(None, "head"),
        ),
        check_vma=False,
    )
```

profile of v0, /device:TPU:0, one launch (start us, length us, event | category | flops | bytes accessed | tf_op | source)
XLA Modules:
  0.0 191.6 jit_solution(12065787987830475894)
XLA Ops:
  7.2 1.9 reshape.213
  12.8 3.0 %collective-permute-start = (bf16[4,128,128]{2,1,0:T(8,128)(2,1)}, bf16[4,128,128]{2,1,0:T(8,128)(2,1)S(1)}, u32[]{:S(2)}, u32[]{:S(2)}) collective-permute-start(bf16[4,128,128]{2,1,0:T(8,128)(2,1)} %convert_element_type.273), channel_id=1, source_target_pairs={{0,4},{4,0},{8,12},{12,8},{16,20},{20,16},{24,28},{28,24},{1,5},{5... | collective-permute-start | bytes 393224 | tf_op jit(solution)/shard_map/ppermute | solution.py:14
  15.8 1.7 reshape.212
  17.6 1.7 reshape_reshape.14
  19.3 1.7 reshape_reshape.15
  26.9 2.0 %fusion.19 = f32[2,1,64,4,128]{4,2,3,1,0:T(8,128)} fusion(f32[2,4,128,64]{2,3,1,0:T(8,128)S(1)} %fusion.128, bf16[2,1,64,4,128]{4,3,2,1,0:T(4,128)(2,1)S(1)} %slice.119, f32[2,2,4,128,128]{4,3,2,1,0:T(8,128)} %bitcast.372), kind=kOutput, calls=%fused_computation.36 | convolution fusion | flops 17367040 | bytes 1179648 | tf_op jit(solution)/shard_map/gjchd,ghde->gjche/dot_general | solution.py:26
  32.0 1.4 reshape.215
  33.5 1.8 concatenate.19.clone
  35.2 1.8 fusion.61
  37.0 1.5 broadcast_multiply_fusion
  39.2 1.6 collective-permute-start.1
  44.2 2.7 %collective-permute-start.2 = (bf16[4,128,128]{2,1,0:T(8,128)(2,1)S(1)}, bf16[4,128,128]{2,1,0:T(8,128)(2,1)S(1)}, u32[]{:S(2)}, u32[]{:S(2)}) collective-permute-start(bf16[4,128,128]{2,1,0:T(8,128)(2,1)S(1)} %fusion.54), channel_id=1, source_target_pairs={{0,16},{4,20},{8,24},{12,28},{16,0},{20,4},{24,8},{28,12},{1,17},{... | collective-permute-start | bytes 393224 | tf_op jit(solution)/shard_map/ppermute | solution.py:14
  48.9 2.9 %collective-permute-done.2 = bf16[4,128,128]{2,1,0:T(8,128)(2,1)S(1)} collective-permute-done((bf16[4,128,128]{2,1,0:T(8,128)(2,1)S(1)}, bf16[4,128,128]{2,1,0:T(8,128)(2,1)S(1)}, u32[]{:S(2)}, u32[]{:S(2)}) %collective-permute-start.2) | collective-permute-done | bytes 131104 | tf_op jit(solution)/shard_map/ppermute | solution.py:14
  53.9 2.0 %convolution_convert_fusion.1 = bf16[256,512]{1,0:T(8,128)(2,1)S(1)} fusion(bf16[256,2048]{1,0:T(8,128)(2,1)} %all-gather.2.cloned.1.call-done, bf16[512,2048]{1,0:T(8,128)(2,1)S(1)} %copy-done), kind=kOutput, calls=%fused_computation.34 | convolution fusion | flops 537001984 | bytes 3407872 | tf_op jit(solution)/shard_map/tj,ij->ti/dot_general | solution.py:108
  55.9 4.5 %fusion.39 = (f32[4,64,4]{1,2,0:T(4,128)}, f32[4,64,4]{1,2,0:T(4,128)}, f32[4,64,4]{1,2,0:T(4,128)}, f32[4,64,4]{1,2,0:T(4,128)}, f32[4,64,4]{1,2,0:T(4,128)}, /...) fusion(f32[4,128,4,64]{1,3,2,0:T(8,128)} %bitcast.385, f32[4,128,4,64]{1,3,2,0:T(8,128)} %bitcast.384, ...), kind=kOutput, calls=%fused_computation.67 | convolution fusion | flops 21620736 | bytes 6078464 | tf_op jit(solution)/shard_map/jhcs,jshe->jche/dot_general | solution.py:21
  60.7 2.7 %multiply_bitcast_fusion = f32[2048,512]{0,1:T(8,128)} fusion(bf16[256,2048]{1,0:T(8,128)(2,1)S(1)} %copy-done.37, bf16[32,8,4,128]{3,2,1,0:T(4,128)(2,1)S(1)} %bitcast.378), kind=kOutput, calls=%fused_computation | convolution fusion | flops 537919488 | bytes 5505024 | tf_op jit(solution)/shard_map/tj,ti->ji/dot_general | solution.py:147
  65.0 1.4 slice_bitcast_fusion.5
  85.7 2.0 %convolution_bitcast_fusion = f32[4,3,128,128]{3,2,1,0:T(8,128)S(1)} fusion(f32[4,64,3,4]{1,0,2,3:T(4,128)} %copy.234, bf16[4,64,4,128,1]{3,2,1,0,4:T(4,128)(2,1)} %bitcast.375, bf16[4,64,4,128]{3,2,1,0:T(4,128)(2,1)S(1)} %reshape.222), kind=kOutput, calls=%fused_computation.5 | convolution fusion | flops 102760448 | bytes 1323008 | tf_op jit(solution)/shard_map/jchd,jclhe->lhde/dot_general | solution.py:26
  87.9 2.1 %fusion.172 = (bf16[3,4,128,128]{2,3,0,1:T(8,128)(2,1)}, f32[3,4,128,128]{2,3,0,1:T(8,128)}) fusion(f32[4,3,128,128]{3,2,1,0:T(8,128)S(1)} %convolution_bitcast_fusion, bf16[4,64,4,128,1]{3,2,1,0,4:T(4,128)(2,1)S(1)} %bitcast.376, f32[4,64,3,4]{1,0,2,3:T(4,128)S(1)} %copy-done.41, bf16[4,64,4,128]{3,2,1,0:T(4,128)(2,1)S(1)} %reshape.222), kind=kOutput, calls=%fused_computation.255 | convolution fusion | flops 101974016 | bytes 2502656 | tf_op jit(solution)/shard_map/jchd,jclhe->lhde/dot_general | solution.py:26
  104.1 1.7 convolution_convert_fusion
  107.1 3.6 %fusion.16 = bf16[4,64,4,128]{3,1,2,0:T(8,128)(2,1)} fusion(f32[4,64,4,128]{3,1,2,0:T(8,128)S(1)} %bitcast.392, f32[4,4,64,128]{3,2,1,0:T(8,128)} %fusion.123, f32[4,128,4,64]{1,3,2,0:T(8,128)} %bitcast.387, f32[4,128,4,64]{1,3,2,0:T(8,128)} %bitcast.386, f32[4,128,4,64]{1,3,2,0:T(8,128)} %bitcast.389, f32[4,128,4,64]{1,3,2,0:T(8,128)} %bitcast.388, ...), kind=kOutput, calls=%fused_computation.31 | convolution fusion | flops 18743296 | bytes 5255168 | tf_op jit(solution)/shard_map/jhcs,jshd->jchd/dot_general | solution.py:21
  115.3 2.1 %copy.275 = f32[2,1,4,128,128]{4,3,2,1,0:T(8,128)} copy(f32[2,1,4,128,128]{3,4,2,0,1:T(8,128)} %fusion.3) | data formatting | bytes 1048576
  117.4 2.1 %concatenate.23.clone = f32[2,2,4,128,128]{4,3,2,1,0:T(8,128)} pad(f32[2,1,4,128,128]{4,3,2,1,0:T(8,128)} %copy.275, f32[]{:T(128)} %constant.16.clone.1), padding=0_0x0_1x0_0x0_0x0_0 | pad | bytes 1572868 | tf_op jit(solution)/shard_map/concatenate | solution.py:54
  119.5 1.8 copy.231
  123.2 21.9 %psum.7 = f32[16,4]{0,1:T(4,128)} all-reduce(f32[16,4]{0,1:T(4,128)S(1)} %fusion.26), channel_id=1, replica_groups=mesh['seq'=8,'head'=4] {'seq'}, use_global_device_ids=true, to_apply=%region_10.0 | all-reduce | flops 64 | bytes 512 | tf_op jit(solution)/shard_map/psum | solution.py:167
  145.1 2.3 %fusion.47 = f32[4,4,128,64]{2,3,1,0:T(8,128)} fusion(f32[4,4,64,64]{3,2,1,0:T(8,128)S(1)} %convolution_multiply_fusion.1, f32[4,4,64]{2,1,0:T(4,128)S(1)} %get-tuple-element.41, bf16[4,64,4,128]{3,2,1,0:T(4,128)(2,1)} %copy-done.3), kind=kOutput, calls=%fused_computation.101 | convolution fusion | flops 16908288 | bytes 1052672 | tf_op jit(solution)/shard_map/jhcs,jche->jshe/dot_general | solution.py:21
  149.6 7.5 %collective-permute-done.5 = bf16[1,4,128,128]{2,3,0,1:T(8,128)(2,1)S(1)} collective-permute-done((bf16[1,4,128,128]{2,3,0,1:T(8,128)(2,1)S(1)}, bf16[1,4,128,128]{2,3,0,1:T(8,128)(2,1)S(1)}, u32[]{:S(2)}, u32[]{:S(2)}) %collective-permute-start.5) | collective-permute-done | bytes 131104 | tf_op jit(solution)/shard_map/ppermute | solution.py:14
  157.1 1.7 fusion.60
  158.9 1.8 copy.237
  161.7 1.6 subtract_convert_fusion
  167.4 2.1 %copy.254 = f32[256,512]{1,0:T(8,128)} copy(f32[256,512]{0,1:T(8,128)} %reduce-scatter.5.cloned.1.call-done) | data formatting | bytes 1048576
  169.5 15.6 %reduce-scatter.3.cloned.1.call-done = bf16[256,512]{1,0:T(8,128)(2,1)} async-done(((bf16[256,2048]{1,0:T(8,128)(2,1)}), bf16[256,512]{1,0:T(8,128)(2,1)}) %reduce-scatter.3.cloned.1.call-update) | async-done | bytes 262160 | tf_op jit(solution)/shard_map/reduce_scatter | solution.py:142
  (227 shorter events, 71.1 us)
Async XLA Ops:
  7.2 46.7 %copy-start = (bf16[512,2048]{1,0:T(8,128)(2,1)S(1)}, bf16[512,2048]{1,0:T(8,128)(2,1)}, u32[]{:S(2)}) copy-start(bf16[512,2048]{1,0:T(8,128)(2,1)} %param.13) | copy-start | bytes 6291460
  7.2 46.7 %all-gather.2.cloned.1.call-start = ((), (), s32[]{:S(2)}) async-start(), calls=%async_computation.3 | async-start | bytes 1310720 | tf_op jit(solution)/shard_map/all_gather | solution.py:107
  11.4 11.6 %copy-start.1 = (f32[4,4,128,128]{3,2,1,0:T(8,128)}, f32[4,4,128,128]{3,2,1,0:T(8,128)S(1)}, u32[]{:S(2)}) copy-start(f32[4,4,128,128]{3,2,1,0:T(8,128)S(1)} %get-tuple-element.51) | copy-start | bytes 3145732
  12.8 26.3 %collective-permute-start = (bf16[4,128,128]{2,1,0:T(8,128)(2,1)}, bf16[4,128,128]{2,1,0:T(8,128)(2,1)S(1)}, u32[]{:S(2)}, u32[]{:S(2)}) collective-permute-start(bf16[4,128,128]{2,1,0:T(8,128)(2,1)} %convert_element_type.273), channel_id=1, source_target_pairs={{0,4},{4,0},{8,12},{12,8},{16,20},{20,16},{24,28},{28,24},{1,5},{5... | collective-permute-start | bytes 393224 | tf_op jit(solution)/shard_map/ppermute | solution.py:14
  15.8 151.6 %reduce-scatter.5.cloned.1.call-start = ((), (), s32[]{:S(2)}) async-start(), calls=%async_computation.4 | async-start | bytes 4718592 | tf_op jit(solution)/shard_map/reduce_scatter | solution.py:146
  25.6 5.7 %copy-start.54 = (s32[256,6]{0,1:T(8,128)S(1)}, s32[256,6]{0,1:T(8,128)}, u32[]{:S(2)}) copy-start(s32[256,6]{0,1:T(8,128)} %param.12) | copy-start | bytes 18436
  25.6 5.7 %copy-start.56 = (f32[16,4]{0,1:T(4,128)S(1)}, f32[16,4]{0,1:T(4,128)}, u32[]{:S(2)}) copy-start(f32[16,4]{0,1:T(4,128)} %param.11) | copy-start | bytes 772
  28.9 8.2 %copy-start.59 = (f32[6]{0:T(128)S(1)}, f32[6]{0:T(128)}, u32[]{:S(2)}) copy-start(f32[6]{0:T(128)} %constant.13.clone) | copy-start | bytes 76
  28.9 10.3 %copy-start.15 = (f32[4,128,128]{2,1,0:T(8,128)S(1)}, f32[4,128,128]{2,1,0:T(8,128)}, u32[]{:S(2)}) copy-start(f32[4,128,128]{2,1,0:T(8,128)} %copy-done.14) | copy-start | bytes 786436
  39.2 5.0 %collective-permute-start.1 = (bf16[4,128,128]{2,1,0:T(8,128)(2,1)S(1)}, bf16[4,128,128]{2,1,0:T(8,128)(2,1)S(1)}, u32[]{:S(2)}, u32[]{:S(2)}) collective-permute-start(bf16[4,128,128]{2,1,0:T(8,128)(2,1)S(1)} %fusion.77), channel_id=1, source_target_pairs={{0,8},{4,12},{8,0},{12,4},{16,24},{20,28},{24,16},{28,20},{1,9},{5... | collective-permute-start | bytes 393224 | tf_op jit(solution)/shard_map/ppermute | solution.py:14
  44.2 3.7 %copy-start.16 = (bf16[4,128,128]{2,1,0:T(8,128)(2,1)}, bf16[4,128,128]{2,1,0:T(8,128)(2,1)S(1)}, u32[]{:S(2)}) copy-start(bf16[4,128,128]{2,1,0:T(8,128)(2,1)S(1)} %collective-permute-done.1) | copy-start | bytes 393220
  44.2 7.6 %collective-permute-start.2 = (bf16[4,128,128]{2,1,0:T(8,128)(2,1)S(1)}, bf16[4,128,128]{2,1,0:T(8,128)(2,1)S(1)}, u32[]{:S(2)}, u32[]{:S(2)}) collective-permute-start(bf16[4,128,128]{2,1,0:T(8,128)(2,1)S(1)} %fusion.54), channel_id=1, source_target_pairs={{0,16},{4,20},{8,24},{12,28},{16,0},{20,4},{24,8},{28,12},{1,17},{... | collective-permute-start | bytes 393224 | tf_op jit(solution)/shard_map/ppermute | solution.py:14
  55.8 4.6 %copy-start.26 = (bf16[256,512]{1,0:T(8,128)(2,1)}, bf16[256,512]{1,0:T(8,128)(2,1)S(1)}, u32[]{:S(2)}) copy-start(bf16[256,512]{1,0:T(8,128)(2,1)S(1)} %convolution_convert_fusion.1) | copy-start | bytes 786436
  55.9 31.9 %copy-start.3 = (bf16[4,64,4,128]{3,2,1,0:T(4,128)(2,1)}, bf16[4,64,4,128]{3,2,1,0:T(4,128)(2,1)S(1)}, u32[]{:S(2)}) copy-start(bf16[4,64,4,128]{3,2,1,0:T(4,128)(2,1)S(1)} %reshape.222) | copy-start | bytes 786436
  55.9 4.7 %copy-start.37 = (bf16[256,2048]{1,0:T(8,128)(2,1)S(1)}, bf16[256,2048]{1,0:T(8,128)(2,1)}, u32[]{:S(2)}) copy-start(bf16[256,2048]{1,0:T(8,128)(2,1)} %all-gather.2.cloned.1.call-done) | copy-start | bytes 3145732
  63.4 4.8 %copy-start.27 = (bf16[256,512]{1,0:T(8,128)(2,1)S(1)}, bf16[256,512]{1,0:T(8,128)(2,1)}, u32[]{:S(2)}) copy-start(bf16[256,512]{1,0:T(8,128)(2,1)} %copy-done.26) | copy-start | bytes 786436
  63.4 121.6 %reduce-scatter.3.cloned.1.call-start = ((), (), s32[]{:S(2)}) async-start(), calls=%async_computation.2 | async-start | bytes 1310720 | tf_op jit(solution)/shard_map/reduce_scatter | solution.py:142
  85.7 5.2 %copy-start.39 = (bf16[2,2,64,4,128]{4,3,2,1,0:T(4,128)(2,1)S(1)}, bf16[2,2,64,4,128]{4,3,2,1,0:T(4,128)(2,1)}, u32[]{:S(2)}) copy-start(bf16[2,2,64,4,128]{4,3,2,1,0:T(4,128)(2,1)} %reshape_reshape.16) | copy-start | bytes 786436
  85.7 5.2 %copy-start.38 = (bf16[1,4,64,4,128]{4,3,2,1,0:T(4,128)(2,1)S(1)}, bf16[1,4,64,4,128]{4,3,2,1,0:T(4,128)(2,1)}, u32[]{:S(2)}) copy-start(bf16[1,4,64,4,128]{4,3,2,1,0:T(4,128)(2,1)} %reshape_reshape.17) | copy-start | bytes 786436
  87.9 3.7 %copy-start.13 = (f32[4,128,128]{2,1,0:T(8,128)S(1)}, f32[4,128,128]{2,1,0:T(8,128)}, u32[]{:S(2)}) copy-start(f32[4,128,128]{2,1,0:T(8,128)} %copy-done.12) | copy-start | bytes 786436
  90.0 4.4 %copy-start.46 = (f32[2,64,4]{1,2,0:T(4,128)S(1)}, f32[2,64,4]{1,2,0:T(4,128)}, u32[]{:S(2)}) copy-start(f32[2,64,4]{1,2,0:T(4,128)} %slice_bitcast_fusion.7) | copy-start | bytes 6148
  90.0 20.6 %collective-permute-start.3 = (bf16[3,4,128,128]{2,3,0,1:T(8,128)(2,1)}, bf16[3,4,128,128]{2,3,0,1:T(8,128)(2,1)}, u32[]{:S(2)}, u32[]{:S(2)}) collective-permute-start(bf16[3,4,128,128]{2,3,0,1:T(8,128)(2,1)} %get-tuple-element.52), channel_id=1, source_target_pairs={{0,4},{4,0},{8,12},{12,8},{16,20},{20,16},{24,28},{28,24},{1,5},{5... | collective-permute-start | bytes 1179656 | tf_op jit(solution)/shard_map/ppermute | solution.py:14
  91.0 11.1 %copy-start.21 = (bf16[2,1,64,4,128]{4,3,2,1,0:T(4,128)(2,1)}, bf16[2,1,64,4,128]{4,3,2,1,0:T(4,128)(2,1)S(1)}, u32[]{:S(2)}) copy-start(bf16[2,1,64,4,128]{4,3,2,1,0:T(4,128)(2,1)S(1)} %slice.131) | copy-start | bytes 393220
  91.2 4.0 %copy-start.57 = (f32[256,6,4]{0,2,1:T(4,128)}, f32[256,6,4]{0,2,1:T(4,128)S(1)}, u32[]{:S(2)}) copy-start(f32[256,6,4]{0,2,1:T(4,128)S(1)} %constant_dynamic-update-slice_fusion) | copy-start | bytes 73732
  91.2 4.0 %copy-start.2 = (f32[4,4,128,128]{3,2,1,0:T(8,128)S(1)}, f32[4,4,128,128]{3,2,1,0:T(8,128)}, u32[]{:S(2)}) copy-start(f32[4,4,128,128]{3,2,1,0:T(8,128)} %copy-done.1) | copy-start | bytes 3145732
  91.8 3.7 %copy-start.30 = (bf16[4,128,128]{2,1,0:T(8,128)(2,1)S(1)}, bf16[4,128,128]{2,1,0:T(8,128)(2,1)}, u32[]{:S(2)}) copy-start(bf16[4,128,128]{2,1,0:T(8,128)(2,1)} %copy-done.29) | copy-start | bytes 393220
  93.1 4.6 %copy-start.17 = (bf16[4,128,128]{2,1,0:T(8,128)(2,1)S(1)}, bf16[4,128,128]{2,1,0:T(8,128)(2,1)}, u32[]{:S(2)}) copy-start(bf16[4,128,128]{2,1,0:T(8,128)(2,1)} %copy-done.16) | copy-start | bytes 393220
  96.6 5.2 %copy-start.4 = (bf16[4,64,4,128]{3,2,1,0:T(4,128)(2,1)S(1)}, bf16[4,64,4,128]{3,2,1,0:T(4,128)(2,1)}, u32[]{:S(2)}) copy-start(bf16[4,64,4,128]{3,2,1,0:T(4,128)(2,1)} %copy-done.3) | copy-start | bytes 786436
  96.6 5.2 %copy-start.40 = (f32[64,64]{1,0:T(8,128)S(1)}, f32[64,64]{1,0:T(8,128)}, u32[]{:S(2)}) copy-start(f32[64,64]{1,0:T(8,128)} %fusion.145) | copy-start | bytes 49156
  107.1 5.6 %copy-start.28 = (f32[3,4,128,128]{2,3,0,1:T(8,128)S(1)}, f32[3,4,128,128]{2,3,0,1:T(8,128)}, u32[]{:S(2)}) copy-start(f32[3,4,128,128]{2,3,0,1:T(8,128)} %get-tuple-element.53) | copy-start | bytes 2359300
  113.7 33.7 %collective-permute-start.4 = (bf16[2,4,128,128]{2,3,0,1:T(8,128)(2,1)}, bf16[2,4,128,128]{2,3,0,1:T(8,128)(2,1)}, u32[]{:S(2)}, u32[]{:S(2)}) collective-permute-start(bf16[2,4,128,128]{2,3,0,1:T(8,128)(2,1)} %get-tuple-element.30), channel_id=1, source_target_pairs={{0,8},{4,12},{8,0},{12,4},{16,24},{20,28},{24,16},{28,20},{1,9},{5... | collective-permute-start | bytes 786440 | tf_op jit(solution)/shard_map/ppermute | solution.py:14
  148.4 8.7 %collective-permute-start.5 = (bf16[1,4,128,128]{2,3,0,1:T(8,128)(2,1)S(1)}, bf16[1,4,128,128]{2,3,0,1:T(8,128)(2,1)S(1)}, u32[]{:S(2)}, u32[]{:S(2)}) collective-permute-start(bf16[1,4,128,128]{2,3,0,1:T(8,128)(2,1)S(1)} %fusion.57), channel_id=1, source_target_pairs={{0,16},{4,20},{8,24},{12,28},{16,0},{20,4},{24,8},{28,12},{1,17},{... | collective-permute-start | bytes 393224 | tf_op jit(solution)/shard_map/ppermute | solution.py:14
  (37 other events, 98.6 us)
Sparse Core Ops, SparseCore 0:
  15.9 17.0 all-gather.1
  63.5 93.6 reduce-scatter.4
  160.3 24.6 reduce-scatter.2
where the time goes:
time: 193 us; the launch traced here: 192 us
  local copies, waits for them, and re-layouts  53.3 us (28%)
  matrix products  53.1 us (28%)
  waiting for transfers between devices  27.4 us (14%)
  blocking collectives  21.9 us (11%)
  between operations  14.5 us (8%)
  other arithmetic  12.5 us (6%)
  starting transfers between devices  8.79 us (5%)
    psum x1, blocking collectives, per_device(): table_grad = lax.psum(table_part, 'seq')  21.9 us
    reduce_scatter x1, waiting for transfers between devices, per_device(): lax.psum_scatter(partial_value.astype(jnp.bfloat16), 'head', scatter_dime...  15.6 us
    unnamed x16, matrix products  14.5 us
    ppermute x6, waiting for transfers between devices, partner_2(): return lax.ppermute(value, axis, pairs)  11.8 us
    dot_general x6, matrix products, split_einsum(): jnp.einsum(form, rest, right, preferred_element_type=jnp.float32)  9.52 us
    ppermute x6, starting transfers between devices, partner_2(): return lax.ppermute(value, axis, pairs)  8.49 us
    another operation x7, local copies, waits for them, and re-layouts, per_device(): jnp.stack([jnp.sum(g_half * level_reads[level_index], axis=3) for level_i...  8.22 us
    unnamed x131, local copies, waits for them, and re-layouts  7.97 us
  transfers between devices with their start and end apart: 9, of which 4 were waited for; matrix products, arithmetic and copies ran while one was open for 53% of the time, Pallas kernels for 0%

commit v1 on v0

--- a/solution.py
+++ b/solution.py
@@ -164,7 +164,7 @@
         )
         * table_norm
     )
-    table_grad = lax.psum(table_part, "seq")
+    table_grad = jnp.sum(jax.lax.all_gather(table_part, axis_name="seq"), 0)
     within_coef = jnp.transpose(level_coef[:, :, 0, :], (0, 2, 1))[:, :, :, None]
     score_grads = (
         jnp.einsum("jche,jshe->jhcs", g_half, v_half, preferred_element_type=jnp.float32)

time: 193 us -> 186 us (0.964)
  waiting for transfers between devices: 27.4 us -> 17.3 us
  blocking collectives: 21.9 us -> 28.4 us
  local copies, waits for them, and re-layouts: 53.3 us -> 48.4 us
    all_gather x0 -> x1, blocking collectives: none -> 28.4 us  [per_device(): table_grad = jnp.sum(jax.lax.all_gather(table_part, axis_name='seq'), 0)]
    psum x1 -> x0, blocking collectives: 21.9 us -> none  [per_device(): table_grad = lax.psum(table_part, 'seq')]
    reduce_scatter x1, waiting for transfers between devices: 15.6 us -> 7.36 us  [per_device(): lax.psum_scatter(partial_value.astype(jnp.bfloat16), 'head', scatter_dime...]
    unnamed x131 -> x125, local copies, waits for them, and re-layouts: 7.97 us -> 7.19 us
  transfers between devices with their start and end apart: 9 -> 9, of which waited for: 4 -> 4; matrix products, arithmetic and copies ran while one was open for 53% -> 54% of each run, Pallas kernels for 0% -> 0%
where the time goes in v1:
time: 186 us; the launch traced here: 184 us
  matrix products  52.5 us (28%)
  local copies, waits for them, and re-layouts  48.4 us (26%)
  blocking collectives  28.4 us (15%)
  waiting for transfers between devices  17.3 us (9%)
  between operations  14.5 us (8%)
  other arithmetic  14.2 us (8%)
  starting transfers between devices  8.85 us (5%)
    all_gather x1, blocking collectives, per_device(): table_grad = jnp.sum(jax.lax.all_gather(table_part, axis_name='seq'), 0)  28.4 us
    unnamed x16, matrix products  14.6 us
    ppermute x6, waiting for transfers between devices, partner_2(): return lax.ppermute(value, axis, pairs)  9.88 us
    dot_general x6, matrix products, split_einsum(): jnp.einsum(form, rest, right, preferred_element_type=jnp.float32)  9.54 us
    ppermute x6, starting transfers between devices, partner_2(): return lax.ppermute(value, axis, pairs)  8.55 us
    another operation x7, local copies, waits for them, and re-layouts, per_device(): jnp.stack([jnp.sum(g_half * level_reads[level_index], axis=3) for level_i...  8.21 us
    reduce_sum x6, local copies, waits for them, and re-layouts, per_device(): jnp.sum(g_half * level_reads[level_index], axis=3)  7.77 us
    reduce_scatter x1, waiting for transfers between devices, per_device(): lax.psum_scatter(partial_value.astype(jnp.bfloat16), 'head', scatter_dime...  7.36 us
  transfers between devices with their start and end apart: 9, of which 4 were waited for; matrix products, arithmetic and copies ran while one was open for 54% of the time, Pallas kernels for 0%

profile of v1, /device:TPU:0, one launch (start us, length us, event | category | flops | bytes accessed | tf_op | source)
XLA Modules:
  0.0 184.2 jit_solution(5064678429881116011)
XLA Ops:
  11.6 3.0 %collective-permute-start = (bf16[4,128,128]{2,1,0:T(8,128)(2,1)}, bf16[4,128,128]{2,1,0:T(8,128)(2,1)S(1)}, u32[]{:S(2)}, u32[]{:S(2)}) collective-permute-start(bf16[4,128,128]{2,1,0:T(8,128)(2,1)} %convert_element_type.273), channel_id=1, source_target_pairs={{0,4},{4,0},{8,12},{12,8},{16,20},{20,16},{24,28},{28,24},{1,5},{5... | collective-permute-start | bytes 393224 | tf_op jit(solution)/shard_map/ppermute | solution.py:14
  22.0 1.4 fusion.129
  23.4 2.0 %fusion.19 = f32[2,1,64,4,128]{4,2,3,1,0:T(8,128)} fusion(f32[2,4,128,64]{2,3,1,0:T(8,128)S(1)} %fusion.129, bf16[2,1,64,4,128]{4,3,2,1,0:T(4,128)(2,1)S(1)} %slice.119, f32[2,2,4,128,128]{4,3,2,1,0:T(8,128)} %bitcast.376), kind=kOutput, calls=%fused_computation.36 | convolution fusion | flops 17367040 | bytes 1179648 | tf_op jit(solution)/shard_map/gjchd,ghde->gjche/dot_general | solution.py:26
  28.4 1.4 reshape.215
  29.9 1.8 concatenate.19.clone
  31.7 1.8 fusion.62
  33.5 1.5 broadcast_multiply_fusion
  35.6 1.5 collective-permute-start.1
  39.2 1.5 collective-permute-done.1
  40.7 2.6 %collective-permute-start.2 = (bf16[4,128,128]{2,1,0:T(8,128)(2,1)S(1)}, bf16[4,128,128]{2,1,0:T(8,128)(2,1)S(1)}, u32[]{:S(2)}, u32[]{:S(2)}) collective-permute-start(bf16[4,128,128]{2,1,0:T(8,128)(2,1)S(1)} %fusion.55), channel_id=1, source_target_pairs={{0,16},{4,20},{8,24},{12,28},{16,0},{20,4},{24,8},{28,12},{1,17},{... | collective-permute-start | bytes 393224 | tf_op jit(solution)/shard_map/ppermute | solution.py:14
  45.3 2.8 %collective-permute-done.2 = bf16[4,128,128]{2,1,0:T(8,128)(2,1)S(1)} collective-permute-done((bf16[4,128,128]{2,1,0:T(8,128)(2,1)S(1)}, bf16[4,128,128]{2,1,0:T(8,128)(2,1)S(1)}, u32[]{:S(2)}, u32[]{:S(2)}) %collective-permute-start.2) | collective-permute-done | bytes 131104 | tf_op jit(solution)/shard_map/ppermute | solution.py:14
  50.2 2.0 %convolution_convert_fusion.1 = bf16[256,512]{1,0:T(8,128)(2,1)S(1)} fusion(bf16[256,2048]{1,0:T(8,128)(2,1)} %all-gather.4.cloned.1.call-done, bf16[512,2048]{1,0:T(8,128)(2,1)S(1)} %copy-done), kind=kOutput, calls=%fused_computation.34 | convolution fusion | flops 537001984 | bytes 3407872 | tf_op jit(solution)/shard_map/tj,ij->ti/dot_general | solution.py:108
  52.3 4.5 %fusion.40 = (f32[4,64,4]{1,2,0:T(4,128)}, f32[4,64,4]{1,2,0:T(4,128)}, f32[4,64,4]{1,2,0:T(4,128)}, f32[4,64,4]{1,2,0:T(4,128)}, f32[4,64,4]{1,2,0:T(4,128)}, /...) fusion(f32[4,128,4,64]{1,3,2,0:T(8,128)} %bitcast.389, f32[4,128,4,64]{1,3,2,0:T(8,128)} %bitcast.388, ...), kind=kOutput, calls=%fused_computation.68 | convolution fusion | flops 21620736 | bytes 6078464 | tf_op jit(solution)/shard_map/jhcs,jshe->jche/dot_general | solution.py:21
  57.1 2.7 %multiply_bitcast_fusion = f32[2048,512]{0,1:T(8,128)} fusion(bf16[256,2048]{1,0:T(8,128)(2,1)S(1)} %copy-done.34, bf16[32,8,4,128]{3,2,1,0:T(4,128)(2,1)S(1)} %bitcast.382), kind=kOutput, calls=%fused_computation | convolution fusion | flops 537919488 | bytes 5505024 | tf_op jit(solution)/shard_map/tj,ti->ji/dot_general | solution.py:147
  61.4 1.4 slice_bitcast_fusion.5
  67.4 1.4 stack.21
  82.1 2.0 %convolution_bitcast_fusion = f32[4,3,128,128]{3,2,1,0:T(8,128)S(1)} fusion(f32[4,64,3,4]{1,0,2,3:T(4,128)} %copy.234, bf16[4,64,4,128,1]{3,2,1,0,4:T(4,128)(2,1)} %bitcast.379, bf16[4,64,4,128]{3,2,1,0:T(4,128)(2,1)S(1)} %reshape.222), kind=kOutput, calls=%fused_computation.5 | convolution fusion | flops 102760448 | bytes 1323008 | tf_op jit(solution)/shard_map/jchd,jclhe->lhde/dot_general | solution.py:26
  84.3 2.1 %fusion.173 = (bf16[3,4,128,128]{2,3,0,1:T(8,128)(2,1)}, f32[3,4,128,128]{2,3,0,1:T(8,128)}) fusion(f32[4,3,128,128]{3,2,1,0:T(8,128)S(1)} %convolution_bitcast_fusion, bf16[4,64,4,128,1]{3,2,1,0,4:T(4,128)(2,1)S(1)} %bitcast.380, f32[4,64,3,4]{1,0,2,3:T(4,128)S(1)} %copy-done.38, bf16[4,64,4,128]{3,2,1,0:T(4,128)(2,1)S(1)} %reshape.222), kind=kOutput, calls=%fused_computation.256 | convolution fusion | flops 101974016 | bytes 2502656 | tf_op jit(solution)/shard_map/jchd,jclhe->lhde/dot_general | solution.py:26
  88.5 1.4 fusion.3
  101.1 1.7 convolution_convert_fusion
  103.9 3.6 %fusion.16 = bf16[4,64,4,128]{3,1,2,0:T(8,128)(2,1)} fusion(f32[4,64,4,128]{3,1,2,0:T(8,128)S(1)} %bitcast.396, f32[4,4,64,128]{3,2,1,0:T(8,128)} %fusion.124, f32[4,128,4,64]{1,3,2,0:T(8,128)} %bitcast.391, f32[4,128,4,64]{1,3,2,0:T(8,128)} %bitcast.390, f32[4,128,4,64]{1,3,2,0:T(8,128)} %bitcast.393, f32[4,128,4,64]{1,3,2,0:T(8,128)} %bitcast.392, ...), kind=kOutput, calls=%fused_computation.31 | convolution fusion | flops 18743296 | bytes 5255168 | tf_op jit(solution)/shard_map/jhcs,jshd->jchd/dot_general | solution.py:21
  110.9 28.4 %all-gather.1 = f32[8,16,4]{1,2,0:T(4,128)S(1)} all-gather(f32[1,16,4]{1,2,0:T(4,128)S(1)} %fusion.27), channel_id=2, replica_groups=mesh['seq'=8,'head'=4] {'seq'}, dimensions={0}, use_global_device_ids=true | all-gather | bytes 2304 | tf_op jit(solution)/shard_map/all_gather | solution.py:167
  139.9 2.0 %copy.275 = f32[2,1,4,128,128]{4,3,2,1,0:T(8,128)} copy(f32[2,1,4,128,128]{3,4,2,0,1:T(8,128)} %fusion.3) | data formatting | bytes 1048576
  141.9 2.1 %concatenate.23.clone = f32[2,2,4,128,128]{4,3,2,1,0:T(8,128)} pad(f32[2,1,4,128,128]{4,3,2,1,0:T(8,128)} %copy.275, f32[]{:T(128)} %constant.16.clone.1), padding=0_0x0_1x0_0x0_0x0_0 | pad | bytes 1572868 | tf_op jit(solution)/shard_map/concatenate | solution.py:54
  144.0 1.8 copy.231
  147.8 2.3 %fusion.48 = f32[4,4,128,64]{2,3,1,0:T(8,128)} fusion(f32[4,4,64,64]{3,2,1,0:T(8,128)S(1)} %convolution_multiply_fusion.1, f32[4,4,64]{2,1,0:T(4,128)S(1)} %get-tuple-element.41, bf16[4,64,4,128]{3,2,1,0:T(4,128)(2,1)} %copy-done.2), kind=kOutput, calls=%fused_computation.102 | convolution fusion | flops 16908288 | bytes 1052672 | tf_op jit(solution)/shard_map/jhcs,jche->jshe/dot_general | solution.py:21
  152.5 5.6 %collective-permute-done.5 = bf16[1,4,128,128]{2,3,0,1:T(8,128)(2,1)S(1)} collective-permute-done((bf16[1,4,128,128]{2,3,0,1:T(8,128)(2,1)S(1)}, bf16[1,4,128,128]{2,3,0,1:T(8,128)(2,1)S(1)}, u32[]{:S(2)}, u32[]{:S(2)}) %collective-permute-start.5) | collective-permute-done | bytes 131104 | tf_op jit(solution)/shard_map/ppermute | solution.py:14
  158.0 1.7 fusion.61
  159.8 1.8 copy.237
  162.6 1.6 subtract_convert_fusion
  168.2 2.1 %copy.254 = f32[256,512]{1,0:T(8,128)} copy(f32[256,512]{0,1:T(8,128)} %reduce-scatter.5.cloned.1.call-done) | data formatting | bytes 1048576
  170.3 7.4 %reduce-scatter.3.cloned.1.call-done = bf16[256,512]{1,0:T(8,128)(2,1)} async-done(((bf16[256,2048]{1,0:T(8,128)(2,1)}), bf16[256,512]{1,0:T(8,128)(2,1)}) %reduce-scatter.3.cloned.1.call-update) | async-done | bytes 262160 | tf_op jit(solution)/shard_map/reduce_scatter | solution.py:142
  (222 shorter events, 69.0 us)
Async XLA Ops:
  7.2 43.1 %copy-start = (bf16[512,2048]{1,0:T(8,128)(2,1)S(1)}, bf16[512,2048]{1,0:T(8,128)(2,1)}, u32[]{:S(2)}) copy-start(bf16[512,2048]{1,0:T(8,128)(2,1)} %param.13) | copy-start | bytes 6291460
  7.2 7.5 %copy-start.23 = (bf16[256,512]{1,0:T(8,128)(2,1)S(1)}, bf16[256,512]{1,0:T(8,128)(2,1)}, u32[]{:S(2)}) copy-start(bf16[256,512]{1,0:T(8,128)(2,1)} %param.8) | copy-start | bytes 786436
  7.2 43.0 %all-gather.4.cloned.1.call-start = ((), (), s32[]{:S(2)}) async-start(), calls=%async_computation.3 | async-start | bytes 1310720 | tf_op jit(solution)/shard_map/all_gather | solution.py:107
  8.4 17.0 %copy-start.5 = (bf16[4,64,4,128]{3,2,1,0:T(4,128)(2,1)}, bf16[4,64,4,128]{3,2,1,0:T(4,128)(2,1)S(1)}, u32[]{:S(2)}) copy-start(bf16[4,64,4,128]{3,2,1,0:T(4,128)(2,1)S(1)} %reshape.213) | copy-start | bytes 786436
  10.9 3.8 %copy-start.14 = (f32[4,128,128]{2,1,0:T(8,128)}, f32[4,128,128]{2,1,0:T(8,128)S(1)}, u32[]{:S(2)}) copy-start(f32[4,128,128]{2,1,0:T(8,128)S(1)} %get-tuple-element.50) | copy-start | bytes 786436
  11.6 23.9 %collective-permute-start = (bf16[4,128,128]{2,1,0:T(8,128)(2,1)}, bf16[4,128,128]{2,1,0:T(8,128)(2,1)S(1)}, u32[]{:S(2)}, u32[]{:S(2)}) collective-permute-start(bf16[4,128,128]{2,1,0:T(8,128)(2,1)} %convert_element_type.273), channel_id=1, source_target_pairs={{0,4},{4,0},{8,12},{12,8},{16,20},{20,16},{24,28},{28,24},{1,5},{5... | collective-permute-start | bytes 393224 | tf_op jit(solution)/shard_map/ppermute | solution.py:14
  14.6 153.6 %reduce-scatter.5.cloned.1.call-start = ((), (), s32[]{:S(2)}) async-start(), calls=%async_computation.4 | async-start | bytes 4718592 | tf_op jit(solution)/shard_map/reduce_scatter | solution.py:146
  14.8 6.2 %copy-start.8 = (bf16[4,64,4,128]{3,2,1,0:T(4,128)(2,1)}, bf16[4,64,4,128]{3,2,1,0:T(4,128)(2,1)S(1)}, u32[]{:S(2)}) copy-start(bf16[4,64,4,128]{3,2,1,0:T(4,128)(2,1)S(1)} %reshape.212) | copy-start | bytes 786436
  17.4 8.0 %copy-start.12 = (f32[4,128,128]{2,1,0:T(8,128)}, f32[4,128,128]{2,1,0:T(8,128)S(1)}, u32[]{:S(2)}) copy-start(f32[4,128,128]{2,1,0:T(8,128)S(1)} %slice_reduce_fusion) | copy-start | bytes 786436
  22.0 5.7 %copy-start.51 = (s32[256,6]{0,1:T(8,128)S(1)}, s32[256,6]{0,1:T(8,128)}, u32[]{:S(2)}) copy-start(s32[256,6]{0,1:T(8,128)} %param.12) | copy-start | bytes 18436
  22.0 5.7 %copy-start.53 = (f32[16,4]{0,1:T(4,128)S(1)}, f32[16,4]{0,1:T(4,128)}, u32[]{:S(2)}) copy-start(f32[16,4]{0,1:T(4,128)} %param.11) | copy-start | bytes 772
  25.4 8.1 %copy-start.56 = (f32[6]{0:T(128)S(1)}, f32[6]{0:T(128)}, u32[]{:S(2)}) copy-start(f32[6]{0:T(128)} %constant.13.clone) | copy-start | bytes 76
  26.6 9.0 %copy-start.15 = (f32[4,128,128]{2,1,0:T(8,128)S(1)}, f32[4,128,128]{2,1,0:T(8,128)}, u32[]{:S(2)}) copy-start(f32[4,128,128]{2,1,0:T(8,128)} %copy-done.14) | copy-start | bytes 786436
  35.6 5.0 %collective-permute-start.1 = (bf16[4,128,128]{2,1,0:T(8,128)(2,1)S(1)}, bf16[4,128,128]{2,1,0:T(8,128)(2,1)S(1)}, u32[]{:S(2)}, u32[]{:S(2)}) collective-permute-start(bf16[4,128,128]{2,1,0:T(8,128)(2,1)S(1)} %fusion.78), channel_id=1, source_target_pairs={{0,8},{4,12},{8,0},{12,4},{16,24},{20,28},{24,16},{28,20},{1,9},{5... | collective-permute-start | bytes 393224 | tf_op jit(solution)/shard_map/ppermute | solution.py:14
  40.6 3.7 %copy-start.16 = (bf16[4,128,128]{2,1,0:T(8,128)(2,1)}, bf16[4,128,128]{2,1,0:T(8,128)(2,1)S(1)}, u32[]{:S(2)}) copy-start(bf16[4,128,128]{2,1,0:T(8,128)(2,1)S(1)} %collective-permute-done.1) | copy-start | bytes 393220
  40.7 7.5 %collective-permute-start.2 = (bf16[4,128,128]{2,1,0:T(8,128)(2,1)S(1)}, bf16[4,128,128]{2,1,0:T(8,128)(2,1)S(1)}, u32[]{:S(2)}, u32[]{:S(2)}) collective-permute-start(bf16[4,128,128]{2,1,0:T(8,128)(2,1)S(1)} %fusion.55), channel_id=1, source_target_pairs={{0,16},{4,20},{8,24},{12,28},{16,0},{20,4},{24,8},{28,12},{1,17},{... | collective-permute-start | bytes 393224 | tf_op jit(solution)/shard_map/ppermute | solution.py:14
  52.2 4.6 %copy-start.24 = (bf16[256,512]{1,0:T(8,128)(2,1)}, bf16[256,512]{1,0:T(8,128)(2,1)S(1)}, u32[]{:S(2)}) copy-start(bf16[256,512]{1,0:T(8,128)(2,1)S(1)} %convolution_convert_fusion.1) | copy-start | bytes 786436
  52.3 31.9 %copy-start.2 = (bf16[4,64,4,128]{3,2,1,0:T(4,128)(2,1)}, bf16[4,64,4,128]{3,2,1,0:T(4,128)(2,1)S(1)}, u32[]{:S(2)}) copy-start(bf16[4,64,4,128]{3,2,1,0:T(4,128)(2,1)S(1)} %reshape.222) | copy-start | bytes 786436
  52.3 4.7 %copy-start.34 = (bf16[256,2048]{1,0:T(8,128)(2,1)S(1)}, bf16[256,2048]{1,0:T(8,128)(2,1)}, u32[]{:S(2)}) copy-start(bf16[256,2048]{1,0:T(8,128)(2,1)} %all-gather.4.cloned.1.call-done) | copy-start | bytes 3145732
  59.8 4.8 %copy-start.25 = (bf16[256,512]{1,0:T(8,128)(2,1)S(1)}, bf16[256,512]{1,0:T(8,128)(2,1)}, u32[]{:S(2)}) copy-start(bf16[256,512]{1,0:T(8,128)(2,1)} %copy-done.24) | copy-start | bytes 786436
  59.8 117.9 %reduce-scatter.3.cloned.1.call-start = ((), (), s32[]{:S(2)}) async-start(), calls=%async_computation.2 | async-start | bytes 1310720 | tf_op jit(solution)/shard_map/reduce_scatter | solution.py:142
  82.1 5.1 %copy-start.36 = (bf16[2,2,64,4,128]{4,3,2,1,0:T(4,128)(2,1)S(1)}, bf16[2,2,64,4,128]{4,3,2,1,0:T(4,128)(2,1)}, u32[]{:S(2)}) copy-start(bf16[2,2,64,4,128]{4,3,2,1,0:T(4,128)(2,1)} %reshape_reshape.16) | copy-start | bytes 786436
  82.1 5.2 %copy-start.35 = (bf16[1,4,64,4,128]{4,3,2,1,0:T(4,128)(2,1)S(1)}, bf16[1,4,64,4,128]{4,3,2,1,0:T(4,128)(2,1)}, u32[]{:S(2)}) copy-start(bf16[1,4,64,4,128]{4,3,2,1,0:T(4,128)(2,1)} %reshape_reshape.17) | copy-start | bytes 786436
  86.4 21.1 %collective-permute-start.3 = (bf16[3,4,128,128]{2,3,0,1:T(8,128)(2,1)}, bf16[3,4,128,128]{2,3,0,1:T(8,128)(2,1)}, u32[]{:S(2)}, u32[]{:S(2)}) collective-permute-start(bf16[3,4,128,128]{2,3,0,1:T(8,128)(2,1)} %get-tuple-element.52), channel_id=1, source_target_pairs={{0,4},{4,0},{8,12},{12,8},{16,20},{20,16},{24,28},{28,24},{1,5},{5... | collective-permute-start | bytes 1179656 | tf_op jit(solution)/shard_map/ppermute | solution.py:14
  88.4 3.7 %copy-start.1 = (f32[4,4,128,128]{3,2,1,0:T(8,128)S(1)}, f32[4,4,128,128]{3,2,1,0:T(8,128)}, u32[]{:S(2)}) copy-start(f32[4,4,128,128]{3,2,1,0:T(8,128)} %get-tuple-element.51) | copy-start | bytes 3145732
  90.3 4.3 %copy-start.17 = (bf16[4,128,128]{2,1,0:T(8,128)(2,1)S(1)}, bf16[4,128,128]{2,1,0:T(8,128)(2,1)}, u32[]{:S(2)}) copy-start(bf16[4,128,128]{2,1,0:T(8,128)(2,1)} %copy-done.16) | copy-start | bytes 393220
  93.5 5.3 %copy-start.3 = (bf16[4,64,4,128]{3,2,1,0:T(4,128)(2,1)S(1)}, bf16[4,64,4,128]{3,2,1,0:T(4,128)(2,1)}, u32[]{:S(2)}) copy-start(bf16[4,64,4,128]{3,2,1,0:T(4,128)(2,1)} %copy-done.2) | copy-start | bytes 786436
  93.5 5.3 %copy-start.37 = (f32[64,64]{1,0:T(8,128)S(1)}, f32[64,64]{1,0:T(8,128)}, u32[]{:S(2)}) copy-start(f32[64,64]{1,0:T(8,128)} %fusion.146) | copy-start | bytes 49156
  103.8 5.5 %copy-start.26 = (f32[3,4,128,128]{2,3,0,1:T(8,128)S(1)}, f32[3,4,128,128]{2,3,0,1:T(8,128)}, u32[]{:S(2)}) copy-start(f32[3,4,128,128]{2,3,0,1:T(8,128)} %get-tuple-element.53) | copy-start | bytes 2359300
  110.4 39.6 %collective-permute-start.4 = (bf16[2,4,128,128]{2,3,0,1:T(8,128)(2,1)}, bf16[2,4,128,128]{2,3,0,1:T(8,128)(2,1)}, u32[]{:S(2)}, u32[]{:S(2)}) collective-permute-start(bf16[2,4,128,128]{2,3,0,1:T(8,128)(2,1)} %get-tuple-element.30), channel_id=1, source_target_pairs={{0,8},{4,12},{8,0},{12,4},{16,24},{20,28},{24,16},{28,20},{1,9},{5... | collective-permute-start | bytes 786440 | tf_op jit(solution)/shard_map/ppermute | solution.py:14
  147.7 3.6 %copy-start.10 = (bf16[4,64,4,128]{3,2,1,0:T(4,128)(2,1)S(1)}, bf16[4,64,4,128]{3,2,1,0:T(4,128)(2,1)}, u32[]{:S(2)}) copy-start(bf16[4,64,4,128]{3,2,1,0:T(4,128)(2,1)} %copy-done.8) | copy-start | bytes 786436
  151.1 7.0 %collective-permute-start.5 = (bf16[1,4,128,128]{2,3,0,1:T(8,128)(2,1)S(1)}, bf16[1,4,128,128]{2,3,0,1:T(8,128)(2,1)S(1)}, u32[]{:S(2)}, u32[]{:S(2)}) collective-permute-start(bf16[1,4,128,128]{2,3,0,1:T(8,128)(2,1)S(1)} %fusion.58), channel_id=1, source_target_pairs={{0,16},{4,20},{8,24},{12,28},{16,0},{20,4},{24,8},{28,12},{1,17},{... | collective-permute-start | bytes 393224 | tf_op jit(solution)/shard_map/ppermute | solution.py:14
  (34 other events, 86.5 us)
Sparse Core Ops, SparseCore 0:
  14.7 17.0 all-gather.3
  59.9 88.4 reduce-scatter.4
  151.6 26.0 reduce-scatter.2
